TPU v7x, 32 devices: a whole 2x2x4 slice. The times are simulated.
32 devices in a mesh: conv: 2 (over x), seq: 8 (over z, y), head: 2 (over core).
Axes of the slice: x: 2, y: 2, z: 4, core: 2. Of those that a mesh axis runs over, the one named last changes fastest.
Arguments:
- queries: bfloat16 [3072, 2048], P(('conv', 'seq'), 'head'), parts along dimension 0, may hold values from -10 to 10, as said below
- key_states: bfloat16 [3072, 512], P(('conv', 'seq'), 'head'), parts along dimension 0, may hold values from -5 to 5, as said below
- value_states: bfloat16 [3072, 512], P(('conv', 'seq'), 'head'), parts along dimension 0, may hold values from -16 to 16
- out_weight: bfloat16 [2048, 4096], P('head'), may hold values from -0.125 to 0.125
- turn_lengths: int32 [32], P('conv'), parts along dimension 0, may hold values from 1 to 959, as said below
- block_flags: int32 [16, 8], P(('conv', 'seq')), parts along dimension 0, may hold values 0 or 1
Outputs:
- pooled: float32 [32, 4096], P(('conv', 'seq'), 'head'), parts along dimension 0
There are 2 independent parts, one for each index of `conv`. A program takes and returns all parts, laid end to end along the dimension named above; an argument that names none is the same for every part. Nothing has to cross between parts.
Inputs may be any that keep to these rules, and one draw needn't show every extreme that they name: `queries`: every entry lies within the stated bounds. `key_states`: every entry lies within the stated bounds. `turn_lengths`: the lengths sum to 1536; turn 0 has one token and turn 1, the longest, has exactly 959 tokens.
All inputs are finite; a program needn't handle non-finite values. No bound on the sum of `block_flags` on one device may be relied on, other than what follows from the above.
Results may differ from a plain program's by a relative error of at most 0.0035.
Values may be sent and summed in bfloat16 or wider, within the bound.
A program may use at most 128 MiB of HBM per device.

v0:
```python
import math
import jax
import jax.numpy as jnp
from jax import lax
from jax.sharding import PartitionSpec as P

HD = 128
big_negative = -1e30
log_two_e = 1.4426950408889634


def on_device(queries, key_states, value_states, out_weight, turn_lengths, block_flags):
    q_rows = queries.shape[0]
    heads_here = queries.shape[1] // HD
    groups = key_states.shape[1] // HD
    repeat = heads_here // groups
    factor = log_two_e / math.sqrt(HD)
    my_index = lax.axis_index("seq")
    own_pos = my_index * q_rows + jnp.arange(q_rows, dtype=jnp.int32)
    block_count = block_flags.shape[1]
    row_pick = jnp.zeros((q_rows,), jnp.int32)
    query_block = own_pos // q_rows
    grouped = queries.reshape(q_rows, groups, repeat, HD)

    def mask_for(key_start, length):
        key_pos = key_start + jnp.arange(length, dtype=jnp.int32)
        key_block = key_pos // q_rows
        hits = key_block[:, None] == jnp.arange(block_count, dtype=jnp.int32)[None, :]
        allowed = jnp.sum(jnp.where(hits[None], block_flags[:, None, :], 0), axis=2)
        allowed_rows = jnp.where(row_pick[:, None] == 1, allowed[-1][None, :], allowed[0][None, :])
        causal = key_pos[None, :] <= own_pos[:, None]
        return causal & ((key_block[None, :] == query_block[:, None]) | (allowed_rows == 1))

    def attend(state, key_rows, value_rows, key_start):
        run_top, run_sum, totals = state
        length = key_rows.shape[0]
        visible = mask_for(key_start, length)[None, None]
        logit = (
            jnp.einsum(
                "qgrd,kgd->grqk",
                grouped,
                key_rows.reshape(length, groups, HD),
                preferred_element_type=jnp.float32,
            )
            * factor
        )
        logit = jnp.where(visible, logit, big_negative)
        new_top = jnp.maximum(run_top, jnp.ceil(jnp.max(logit, axis=-1)))
        weights = jnp.where(visible, jnp.exp2(logit - new_top[..., None]), 0.0)
        rescale = jnp.exp2(run_top - new_top)
        run_sum = run_sum * rescale + jnp.sum(weights, axis=-1)
        update = jnp.einsum(
            "grqk,kgd->grqd",
            weights.astype(jnp.bfloat16),
            value_rows.reshape(length, groups, HD),
            preferred_element_type=jnp.float32,
        )
        totals = totals * rescale[..., None] + update
        return (new_top, run_sum, totals)

    start_state = (
        jnp.full((groups, repeat, q_rows), big_negative, jnp.float32),
        jnp.zeros((groups, repeat, q_rows), jnp.float32),
        jnp.zeros((groups, repeat, q_rows, HD), jnp.float32),
    )
    key_piece = lax.all_gather(key_states, "seq", axis=0, tiled=True)
    value_piece = lax.all_gather(value_states, "seq", axis=0, tiled=True)
    length = key_piece.shape[0]
    width_step = math.gcd(length, 1024)

    def one_block(number, carried):
        offset = number * width_step
        key_rows = lax.dynamic_slice_in_dim(key_piece, offset, width_step, 0)
        value_rows = lax.dynamic_slice_in_dim(value_piece, offset, width_step, 0)
        return attend(carried, key_rows, value_rows, offset)

    run_top, run_sum, totals = lax.fori_loop(0, length // width_step, one_block, start_state)
    attended_work = (
        (totals / run_sum[..., None])
        .transpose(2, 0, 1, 3)
        .reshape(q_rows, heads_here * HD)
        .astype(jnp.bfloat16)
    )
    turn_ends = jnp.cumsum(turn_lengths)
    starts = turn_ends - turn_lengths
    member = (starts[:, None] <= own_pos[None, :]) & (own_pos[None, :] < turn_ends[:, None])
    turn_share = jnp.where(member, 1.0, 0.0).astype(jnp.float32) / turn_lengths[:, None].astype(
        jnp.float32
    )
    partial_rows = jnp.dot(attended_work, out_weight, preferred_element_type=jnp.float32)
    projected_rows = lax.psum_scatter(partial_rows, "head", scatter_dimension=1, tiled=True)
    pooled_part = jnp.dot(turn_share, projected_rows, precision=lax.Precision.HIGHEST)
    return lax.psum_scatter(pooled_part, "seq", scatter_dimension=0, tiled=True)


def solution(mesh):
    in_specs = (
        P(("conv", "seq"), "head"),
        P(("conv", "seq"), "head"),
        P(("conv", "seq"), "head"),
        P("head", None),
        P("conv"),
        P(("conv", "seq"), None),
    )
    out_specs = P(("conv", "seq"), "head")
    return jax.shard_map(
        on_device, mesh=mesh, in_specs=in_specs, out_specs=out_specs, check_vma=False
    )
```

profile of v0, /device:TPU:0, one launch (start us, length us, event | category | flops | bytes accessed | tf_op | source)
XLA Modules:
  0.0 211.3 jit_solution(6904133844643909026)
XLA Ops:
  6.5 36.3 %all_gather.6 = bf16[1536,256]{1,0:T(8,128)(2,1)} all-gather(bf16[192,256]{1,0:T(8,128)(2,1)} %param.9), channel_id=1, replica_groups=mesh['conv'=2,'seq'=8,'head'=2] {'seq'}, dimensions={0}, use_global_device_ids=true | all-gather | bytes 884736 | tf_op jit(solution)/shard_map/all_gather | solution.py:66
  42.9 34.2 %all_gather.7 = bf16[1536,256]{1,0:T(8,128)(2,1)} all-gather(bf16[192,256]{1,0:T(8,128)(2,1)} %param.10), channel_id=1, replica_groups=mesh['conv'=2,'seq'=8,'head'=2] {'seq'}, dimensions={0}, use_global_device_ids=true | all-gather | bytes 884736 | tf_op jit(solution)/shard_map/all_gather | solution.py:67
  77.1 1.3 reshape.229
  79.2 28.0 %while.22 = (s32[]{:T(128)}, f32[2,4,192]{2,1,0:T(4,128)S(1)}, f32[2,4,192]{2,1,0:T(4,128)S(1)}, f32[2,4,192,128]{3,2,1,0:T(8,128)}, s32[1,8]{1,0:T(1,128)S(1)},...) while((s32[]{:T(128)}, f32[2,4,192]{2,1,0:T(4,128)S(1)}, ...), condition=%wide.region_5.6_spmd.clone.clone.clone, body=%wide.region_1.5_spmd.clone.clone.clone.sunk | while | flops 415462080 | bytes 14534883 | solution.py:77
  79.5 1.1 constant_dynamic-slice_fusion.4
  81.4 1.8 fusion.54
  83.3 1.2 fusion.55
  84.5 0.8 copy.40
  85.3 3.1 %fusion.57 = f32[2,4,192,128]{3,2,1,0:T(8,128)} fusion(bf16[512,2,128,1]{0,2,3,1:T(8,128)(2,1)} %bitcast.53, f32[2,512,192,4]{1,2,3,0:T(8,128)S(1)} %get-tuple-element.465, f32[2,4,192]{2,1,0:T(4,128)S(1)} %ceil_maximum_fusion.2, pred[192,512]{1,0:T(8,128)(4,1)S(1)} %or_and_fusion.2, f32[2,4,192,128]{3,2,1,0:T(8,128)} %get-tuple-element.485, ...), kind=kOutput, calls=%fused_computation.9.clone.1 | convolution fusion | flops 206635008 | bytes 5091329 | tf_op jit(solution)/shard_map/while/body/eval_jaxpr/grqk,kgd->grqd/dot_general | solution.py:52
  88.8 1.1 constant_dynamic-slice_fusion.4
  90.7 1.8 fusion.54
  92.5 1.2 fusion.55
  93.8 0.8 copy.40
  94.6 3.2 %fusion.57 = f32[2,4,192,128]{3,2,1,0:T(8,128)} fusion(bf16[512,2,128,1]{0,2,3,1:T(8,128)(2,1)} %bitcast.53, f32[2,512,192,4]{1,2,3,0:T(8,128)S(1)} %get-tuple-element.465, f32[2,4,192]{2,1,0:T(4,128)S(1)} %ceil_maximum_fusion.2, pred[192,512]{1,0:T(8,128)(4,1)S(1)} %or_and_fusion.2, f32[2,4,192,128]{3,2,1,0:T(8,128)} %get-tuple-element.485, ...), kind=kOutput, calls=%fused_computation.9.clone.1 | convolution fusion | flops 206635008 | bytes 5091329 | tf_op jit(solution)/shard_map/while/body/eval_jaxpr/grqk,kgd->grqd/dot_general | solution.py:52
  98.1 1.1 constant_dynamic-slice_fusion.4
  100.1 1.8 fusion.54
  101.9 1.2 fusion.55
  104.0 3.2 %fusion.57 = f32[2,4,192,128]{3,2,1,0:T(8,128)} fusion(bf16[512,2,128,1]{0,2,3,1:T(8,128)(2,1)} %bitcast.53, f32[2,512,192,4]{1,2,3,0:T(8,128)S(1)} %get-tuple-element.465, f32[2,4,192]{2,1,0:T(4,128)S(1)} %ceil_maximum_fusion.2, pred[192,512]{1,0:T(8,128)(4,1)S(1)} %or_and_fusion.2, f32[2,4,192,128]{3,2,1,0:T(8,128)} %get-tuple-element.485, ...), kind=kOutput, calls=%fused_computation.9.clone.1 | convolution fusion | flops 206635008 | bytes 5091329 | tf_op jit(solution)/shard_map/while/body/eval_jaxpr/grqk,kgd->grqd/dot_general | solution.py:52
  107.2 1.4 fusion.19
  109.2 6.9 %fusion.35 = f32[192,4096]{1,0:T(8,128)} fusion(bf16[192,1024]{1,0:T(8,128)(2,1)S(1)} %convert_element_type.26, bf16[1024,4096]{1,0:T(8,128)(2,1)} %param.11), kind=kOutput, calls=%fused_computation.51 | convolution fusion | flops 1610612736 | bytes 11927552 | tf_op jit(solution)/shard_map/dot_general | solution.py:90
  117.0 11.5 %reduce-scatter.2.cloned.1.call-done = f32[192,2048]{1,0:T(8,128)} async-done(((f32[192,4096]{1,0:T(8,128)}), f32[192,2048]{1,0:T(8,128)}) %reduce-scatter.2.cloned.1.call-update) | async-done | bytes 1572880 | tf_op jit(solution)/shard_map/reduce_scatter | solution.py:91
  128.5 2.9 %fusion.20 = f32[16,2048]{1,0:T(8,128)} fusion(f32[192,2048]{1,0:T(8,128)} %reduce-scatter.2.cloned.1.call-done, f32[16]{0:T(128)S(1)} %get-tuple-element.393, s32[192]{0:T(256)S(1)} %iota_add_fusion.2, s32[16]{0:T(128)S(1)} %reduce.6, s32[16]{0:T(128)S(1)} %get-tuple-element.392), kind=kOutput, calls=%fused_computation.34 | convolution fusion | flops 75512832 | bytes 1704896 | tf_op jit(solution)/shard_map/dot_general | solution.py:92
  132.6 70.4 %all-reduce.3.cloned.1.call-done = f32[16,2048]{1,0:T(8,128)} async-done(((f32[16,2048]{1,0:T(8,128)}), f32[16,2048]{1,0:T(8,128)}) %all-reduce.3.cloned.1.call-update) | async-done | bytes 131088
  203.0 1.5 constant_dynamic-slice_fusion.2
  (50 shorter events, 7.2 us)
Async XLA Ops:
  6.5 72.6 %copy-start = (s32[1,8]{1,0:T(1,128)S(1)}, s32[1,8]{1,0:T(1,128)}, u32[]{:S(2)}) copy-start(s32[1,8]{1,0:T(1,128)} %param.13) | copy-start | bytes 100
  6.5 121.9 %reduce-scatter.2.cloned.1.call-start = ((), (), s32[]{:S(2)}) async-start(), calls=%async_computation.1 | async-start | bytes 4718592 | tf_op jit(solution)/shard_map/reduce_scatter | solution.py:91
  116.1 0.7 copy-start.1
  116.1 15.3 %copy-start.2 = (u32[32]{0:T(128)S(1)}, u32[32]{0:T(128)}, u32[]{:S(2)}) copy-start(u32[32]{0:T(128)} %constant.141) | copy-start | bytes 388
  116.1 86.9 %all-reduce.3.cloned.1.call-start = ((), (), s32[]{:S(2)}) async-start(), calls=%async_computation.2 | async-start | bytes 262144
Sparse Core Ops, SparseCore 0:
  116.2 12.2 reduce-scatter.1
  132.2 70.7 all-reduce.2
where the time goes:
time: 212 us; the launch traced here: 211 us
  waiting for transfers between devices  81.9 us (39%)
  blocking collectives  70.6 us (33%)
  matrix products  24.8 us (12%)
  between operations  14.1 us (7%)
  local copies, waits for them, and re-layouts  13.6 us (6%)
  other arithmetic  6.13 us (3%)
    unnamed x3, waiting for transfers between devices  70.4 us
    all_gather x1, blocking collectives, on_device(): key_piece = lax.all_gather(key_states, 'seq', axis=0, tiled=True)  36.3 us
    all_gather x1, blocking collectives, on_device(): value_piece = lax.all_gather(value_states, 'seq', axis=0, tiled=True)  34.2 us
    reduce_scatter x1, waiting for transfers between devices, on_device(): lax.psum_scatter(partial_rows, 'head', scatter_dimension=1, tiled=True)  11.5 us
    dot_general x3, matrix products, attend(): jnp.einsum('grqk,kgd->grqd', weights.astype(jnp.bfloat16), value_rows.res...  9.53 us
    dot_general x1, matrix products, on_device(): jnp.dot(attended_work, out_weight, preferred_element_type=jnp.float32)  6.85 us
    dynamic_slice x6, local copies, waits for them, and re-layouts, one_block(): value_rows = lax.dynamic_slice_in_dim(value_piece, offset, width_step, 0)  5.76 us
    dot_general x3, matrix products, attend(): jnp.einsum('qgrd,kgd->grqk', grouped, key_rows.reshape(length, groups, HD...  5.5 us
  transfers between devices with their start and end apart: 2, of which 2 were waited for; matrix products, arithmetic and copies ran while one was open for 0% of the time, Pallas kernels for 0%

commit v1 on v0

--- a/solution.py
+++ b/solution.py
@@ -7,6 +7,18 @@
 HD = 128
 big_negative = -1e30
 log_two_e = 1.4426950408889634
+
+
+def gather_by_bits(array, axis, dim):
+    ways, here = (lax.axis_size(axis), lax.axis_index(axis))
+    grown, reach = (array, 1)
+    while reach < ways:
+        theirs = lax.ppermute(grown, axis, [(d, d ^ reach) for d in range(ways)])
+        mine_first = jnp.concatenate([grown, theirs], axis=dim)
+        theirs_first = jnp.concatenate([theirs, grown], axis=dim)
+        grown = jnp.where(here & reach == 0, mine_first, theirs_first)
+        reach = 2 * reach
+    return grown
 
 
 def on_device(queries, key_states, value_states, out_weight, turn_lengths, block_flags):
@@ -63,7 +75,7 @@
         jnp.zeros((groups, repeat, q_rows), jnp.float32),
         jnp.zeros((groups, repeat, q_rows, HD), jnp.float32),
     )
-    key_piece = lax.all_gather(key_states, "seq", axis=0, tiled=True)
+    key_piece = gather_by_bits(key_states, "seq", 0)
     value_piece = lax.all_gather(value_states, "seq", axis=0, tiled=True)
     length = key_piece.shape[0]
     width_step = math.gcd(length, 1024)

time: 212 us -> 195 us (0.920)
  blocking collectives: 70.6 us -> 40.4 us
  starting transfers between devices: 0.04 us -> 7.49 us
  waiting for transfers between devices: 81.9 us -> 85.5 us
    all_gather x1 -> x0, blocking collectives: 36.3 us -> none  [on_device(): key_piece = lax.all_gather(key_states, 'seq', axis=0, tiled=True)]
    ppermute x0 -> x3, waiting for transfers between devices: none -> 7.79 us  [gather_by_bits(): theirs = lax.ppermute(grown, axis, [(d, d ^ reach) for d in range(ways)])]
    ppermute x0 -> x3, starting transfers between devices: none -> 7.45 us  [gather_by_bits(): theirs = lax.ppermute(grown, axis, [(d, d ^ reach) for d in range(ways)])]
    all_gather x1, blocking collectives: 34.2 us -> 40.4 us  [on_device(): value_piece = lax.all_gather(value_states, 'seq', axis=0, tiled=True)]
    reduce_scatter x1, waiting for transfers between devices: 11.5 us -> 7.25 us  [on_device(): lax.psum_scatter(partial_rows, 'head', scatter_dimension=1, tiled=True)]
    unnamed x9 -> x10, local copies, waits for them, and re-layouts: 3.42 us -> 4.42 us
  transfers between devices with their start and end apart: 2 -> 5, of which waited for: 2 -> 4; matrix products, arithmetic and copies ran while one was open for 0% -> 1% of each run, Pallas kernels for 0% -> 0%
where the time goes in v1:
time: 195 us; the launch traced here: 194 us
  waiting for transfers between devices  85.5 us (44%)
  blocking collectives  40.4 us (21%)
  matrix products  24.6 us (13%)
  local copies, waits for them, and re-layouts  14.7 us (8%)
  between operations  14.1 us (7%)
  starting transfers between devices  7.49 us (4%)
  other arithmetic  7.44 us (4%)
    unnamed x3, waiting for transfers between devices  70.4 us
    all_gather x1, blocking collectives, on_device(): value_piece = lax.all_gather(value_states, 'seq', axis=0, tiled=True)  40.4 us
    dot_general x3, matrix products, attend(): jnp.einsum('grqk,kgd->grqd', weights.astype(jnp.bfloat16), value_rows.res...  9.53 us
    ppermute x3, waiting for transfers between devices, gather_by_bits(): theirs = lax.ppermute(grown, axis, [(d, d ^ reach) for d in range(ways)])  7.79 us
    ppermute x3, starting transfers between devices, gather_by_bits(): theirs = lax.ppermute(grown, axis, [(d, d ^ reach) for d in range(ways)])  7.45 us
    reduce_scatter x1, waiting for transfers between devices, on_device(): lax.psum_scatter(partial_rows, 'head', scatter_dimension=1, tiled=True)  7.25 us
    dot_general x1, matrix products, on_device(): jnp.dot(attended_work, out_weight, preferred_element_type=jnp.float32)  6.85 us
    dynamic_slice x6, local copies, waits for them, and re-layouts, one_block(): value_rows = lax.dynamic_slice_in_dim(value_piece, offset, width_step, 0)  5.46 us
  transfers between devices with their start and end apart: 5, of which 4 were waited for; matrix products, arithmetic and copies ran while one was open for 1% of the time, Pallas kernels for 0%

profile of v1, /device:TPU:0, one launch (start us, length us, event | category | flops | bytes accessed | tf_op | source)
XLA Modules:
  0.0 194.4 jit_solution(6553951902228426111)
XLA Ops:
  7.5 3.0 %collective-permute-start = (bf16[192,256]{0,1:T(8,128)(2,1)S(1)}, bf16[192,256]{0,1:T(8,128)(2,1)S(1)}, u32[]{:S(2)}, u32[]{:S(2)}) collective-permute-start(bf16[192,256]{0,1:T(8,128)(2,1)S(1)} %copy.30), channel_id=1, source_target_pairs={{0,2},{2,0},{4,6},{6,4},{8,10},{10,8},{12,14},{14,12},{1,3},{3,1},... | collective-permute-start | bytes 294920 | tf_op jit(solution)/shard_map/ppermute | solution.py:16
  10.6 3.5 %collective-permute-done = bf16[192,256]{0,1:T(8,128)(2,1)S(1)} collective-permute-done((bf16[192,256]{0,1:T(8,128)(2,1)S(1)}, bf16[192,256]{0,1:T(8,128)(2,1)S(1)}, u32[]{:S(2)}, u32[]{:S(2)}) %collective-permute-start) | collective-permute-done | bytes 98336 | tf_op jit(solution)/shard_map/ppermute | solution.py:16
  14.2 1.9 collective-permute-start.1
  16.1 4.3 %collective-permute-done.1 = bf16[384,256]{0,1:T(8,128)(2,1)S(1)} collective-permute-done((bf16[384,256]{0,1:T(8,128)(2,1)S(1)}, bf16[384,256]{0,1:T(8,128)(2,1)S(1)}, u32[]{:S(2)}, u32[]{:S(2)}) %collective-permute-start.1) | collective-permute-done | bytes 196640 | tf_op jit(solution)/shard_map/ppermute | solution.py:16
  20.5 2.6 %collective-permute-start.2 = (bf16[768,256]{0,1:T(8,128)(2,1)S(1)}, bf16[768,256]{0,1:T(8,128)(2,1)S(1)}, u32[]{:S(2)}, u32[]{:S(2)}) collective-permute-start(bf16[768,256]{0,1:T(8,128)(2,1)S(1)} %maximum_select_fusion.1), channel_id=1, source_target_pairs={{0,8},{2,10},{4,12},{6,14},{8,0},{10,2},{12,4},{14,6},{1,9},{3,11}... | collective-permute-start | bytes 1179656 | tf_op jit(solution)/shard_map/ppermute | solution.py:16
  23.1 1.3 reshape.229
  25.1 40.4 %all_gather.3 = bf16[1536,256]{1,0:T(8,128)(2,1)} all-gather(bf16[192,256]{1,0:T(8,128)(2,1)} %param.10), channel_id=1, replica_groups=mesh['conv'=2,'seq'=8,'head'=2] {'seq'}, dimensions={0}, use_global_device_ids=true | all-gather | bytes 884736 | tf_op jit(solution)/shard_map/all_gather | solution.py:79
  65.5 1.1 maximum_select_fusion
  66.6 27.9 %while.22 = (s32[]{:T(128)}, f32[2,4,192]{2,1,0:T(4,128)S(1)}, f32[2,4,192]{2,1,0:T(4,128)S(1)}, f32[2,4,192,128]{3,2,1,0:T(8,128)}, s32[1,8]{1,0:T(1,128)S(1)},...) while((s32[]{:T(128)}, f32[2,4,192]{2,1,0:T(4,128)S(1)}, ...), condition=%wide.region_5.6_spmd.clone.clone.clone, body=%wide.region_1.5_spmd.clone.clone.clone.sunk | while | flops 415462080 | bytes 14010599 | solution.py:89
  67.9 1.8 fusion.54
  69.7 1.2 fusion.55
  72.7 3.1 %fusion.57 = f32[2,4,192,128]{3,2,1,0:T(8,128)} fusion(bf16[512,2,128,1]{0,2,3,1:T(8,128)(2,1)} %bitcast.53, f32[2,512,192,4]{1,2,3,0:T(8,128)S(1)} %get-tuple-element.460, f32[2,4,192]{2,1,0:T(4,128)S(1)} %ceil_maximum_fusion.2, pred[192,512]{1,0:T(8,128)(4,1)S(1)} %or_and_fusion.2, f32[2,4,192,128]{3,2,1,0:T(8,128)} %get-tuple-element.479, ...), kind=kOutput, calls=%fused_computation.9.clone.1 | convolution fusion | flops 206635008 | bytes 5091329 | tf_op jit(solution)/shard_map/while/body/eval_jaxpr/grqk,kgd->grqd/dot_general | solution.py:64
  77.1 1.8 fusion.54
  78.9 1.2 fusion.55
  82.0 3.2 %fusion.57 = f32[2,4,192,128]{3,2,1,0:T(8,128)} fusion(bf16[512,2,128,1]{0,2,3,1:T(8,128)(2,1)} %bitcast.53, f32[2,512,192,4]{1,2,3,0:T(8,128)S(1)} %get-tuple-element.460, f32[2,4,192]{2,1,0:T(4,128)S(1)} %ceil_maximum_fusion.2, pred[192,512]{1,0:T(8,128)(4,1)S(1)} %or_and_fusion.2, f32[2,4,192,128]{3,2,1,0:T(8,128)} %get-tuple-element.479, ...), kind=kOutput, calls=%fused_computation.9.clone.1 | convolution fusion | flops 206635008 | bytes 5091329 | tf_op jit(solution)/shard_map/while/body/eval_jaxpr/grqk,kgd->grqd/dot_general | solution.py:64
  86.5 1.8 fusion.54
  88.2 1.2 fusion.55
  91.3 3.2 %fusion.57 = f32[2,4,192,128]{3,2,1,0:T(8,128)} fusion(bf16[512,2,128,1]{0,2,3,1:T(8,128)(2,1)} %bitcast.53, f32[2,512,192,4]{1,2,3,0:T(8,128)S(1)} %get-tuple-element.460, f32[2,4,192]{2,1,0:T(4,128)S(1)} %ceil_maximum_fusion.2, pred[192,512]{1,0:T(8,128)(4,1)S(1)} %or_and_fusion.2, f32[2,4,192,128]{3,2,1,0:T(8,128)} %get-tuple-element.479, ...), kind=kOutput, calls=%fused_computation.9.clone.1 | convolution fusion | flops 206635008 | bytes 5091329 | tf_op jit(solution)/shard_map/while/body/eval_jaxpr/grqk,kgd->grqd/dot_general | solution.py:64
  94.5 1.4 fusion.19
  96.5 6.9 %fusion.35 = f32[192,4096]{1,0:T(8,128)} fusion(bf16[192,1024]{1,0:T(8,128)(2,1)S(1)} %convert_element_type.26, bf16[1024,4096]{1,0:T(8,128)(2,1)} %param.11), kind=kOutput, calls=%fused_computation.54 | convolution fusion | flops 1610612736 | bytes 11927552 | tf_op jit(solution)/shard_map/dot_general | solution.py:102
  104.3 7.3 %reduce-scatter.2.cloned.1.call-done = f32[192,2048]{1,0:T(8,128)} async-done(((f32[192,4096]{1,0:T(8,128)}), f32[192,2048]{1,0:T(8,128)}) %reduce-scatter.2.cloned.1.call-update) | async-done | bytes 1572880 | tf_op jit(solution)/shard_map/reduce_scatter | solution.py:103
  111.5 2.9 %fusion.20 = f32[16,2048]{1,0:T(8,128)} fusion(f32[192,2048]{1,0:T(8,128)} %reduce-scatter.2.cloned.1.call-done, f32[16]{0:T(128)S(1)} %get-tuple-element.391, s32[192]{0:T(256)S(1)} %iota_add_fusion.2, s32[16]{0:T(128)S(1)} %reduce.6, s32[16]{0:T(128)S(1)} %get-tuple-element.390), kind=kOutput, calls=%fused_computation.37 | convolution fusion | flops 75512832 | bytes 1704896 | tf_op jit(solution)/shard_map/dot_general | solution.py:104
  115.7 70.4 %all-reduce.3.cloned.1.call-done = f32[16,2048]{1,0:T(8,128)} async-done(((f32[16,2048]{1,0:T(8,128)}), f32[16,2048]{1,0:T(8,128)}) %all-reduce.3.cloned.1.call-update) | async-done | bytes 131088
  186.1 1.5 constant_dynamic-slice_fusion.2
  (59 shorter events, 13.5 us)
Async XLA Ops:
  6.5 60.1 %copy-start = (s32[1,8]{1,0:T(1,128)S(1)}, s32[1,8]{1,0:T(1,128)}, u32[]{:S(2)}) copy-start(s32[1,8]{1,0:T(1,128)} %param.13) | copy-start | bytes 100
  6.5 105.0 %reduce-scatter.2.cloned.1.call-start = ((), (), s32[]{:S(2)}) async-start(), calls=%async_computation.1 | async-start | bytes 4718592 | tf_op jit(solution)/shard_map/reduce_scatter | solution.py:103
  7.5 6.5 %collective-permute-start = (bf16[192,256]{0,1:T(8,128)(2,1)S(1)}, bf16[192,256]{0,1:T(8,128)(2,1)S(1)}, u32[]{:S(2)}, u32[]{:S(2)}) collective-permute-start(bf16[192,256]{0,1:T(8,128)(2,1)S(1)} %copy.30), channel_id=1, source_target_pairs={{0,2},{2,0},{4,6},{6,4},{8,10},{10,8},{12,14},{14,12},{1,3},{3,1},... | collective-permute-start | bytes 294920 | tf_op jit(solution)/shard_map/ppermute | solution.py:16
  14.2 6.2 %collective-permute-start.1 = (bf16[384,256]{0,1:T(8,128)(2,1)S(1)}, bf16[384,256]{0,1:T(8,128)(2,1)S(1)}, u32[]{:S(2)}, u32[]{:S(2)}) collective-permute-start(bf16[384,256]{0,1:T(8,128)(2,1)S(1)} %maximum_select_fusion.2), channel_id=1, source_target_pairs={{0,4},{2,6},{4,0},{6,2},{8,12},{10,14},{12,8},{14,10},{1,5},{3,7},... | collective-permute-start | bytes 589832 | tf_op jit(solution)/shard_map/ppermute | solution.py:16
  20.5 45.1 %collective-permute-start.2 = (bf16[768,256]{0,1:T(8,128)(2,1)S(1)}, bf16[768,256]{0,1:T(8,128)(2,1)S(1)}, u32[]{:S(2)}, u32[]{:S(2)}) collective-permute-start(bf16[768,256]{0,1:T(8,128)(2,1)S(1)} %maximum_select_fusion.1), channel_id=1, source_target_pairs={{0,8},{2,10},{4,12},{6,14},{8,0},{10,2},{12,4},{14,6},{1,9},{3,11}... | collective-permute-start | bytes 1179656 | tf_op jit(solution)/shard_map/ppermute | solution.py:16
  103.4 0.7 copy-start.1
  103.4 11.1 %copy-start.2 = (u32[32]{0:T(128)S(1)}, u32[32]{0:T(128)}, u32[]{:S(2)}) copy-start(u32[32]{0:T(128)} %constant.146) | copy-start | bytes 388
  103.4 82.7 %all-reduce.3.cloned.1.call-start = ((), (), s32[]{:S(2)}) async-start(), calls=%async_computation.2 | async-start | bytes 262144
Sparse Core Ops, SparseCore 0:
  103.5 7.9 reduce-scatter.1
  115.2 70.8 all-reduce.2
